TPU v7x, 512 devices: a whole 4x4x16 slice. The times are simulated.
512 devices in a mesh: dp: 64 (over x, y, z_hi, core), shard: 8 (over z_lo).
Axes of the slice: x: 4, y: 4, z: 16 (z_hi: 2, z_lo: 8; z = z_hi * 8 + z_lo), core: 2. Of those that a mesh axis runs over, the one named last changes fastest.
Arguments:
- group_grads: bfloat16 [64, 1024, 1024], P('dp', 'shard'), may hold values from -2 to 2
- moment: float32 [1024, 1024], P('shard'), may hold values from -6 to 6
- second: float32 [1024, 1024], P(None, 'shard'), may hold values from 0.5 to 4
- stat_left: float32 [1024, 1024], P('shard'), may hold values from -200 to 2000, as said below
- stat_right: float32 [1024, 1024], P('shard'), may hold values from -200 to 2000, as said below
- basis_left: float32 [1024, 1024], P('shard'), as said below
- basis_right: float32 [1024, 1024], P('shard'), as said below
Outputs:
- update: bfloat16 [1024, 1024], P('shard')
- second_new: float32 [1024, 1024], P(None, 'shard')
- left_new: float32 [1024, 1024], P('shard')
- right_new: float32 [1024, 1024], P('shard')
Inputs may be any that keep to these rules, and one draw needn't show every extreme that they name: `stat_left`: each statistic is symmetric. `stat_right`: each statistic is symmetric. `basis_left`: diagonal entries near 0.9 sqrt(1024), off-diagonal entries of order one. `basis_right`: diagonal entries near 0.9 sqrt(1024), off-diagonal entries of order one.
All inputs are finite; a program needn't handle non-finite values.
Results may differ from a plain program's by a relative error of at most 0.0049.
The roundings to bfloat16 on the way count: a program that leaves them out, or rounds other values in their place, can miss the bound.
Values may be sent and summed in bfloat16 or wider, within the bound.
A program may use at most 128 MiB of HBM per device.

v0:
```python
import jax
import jax.numpy as jnp
from jax import lax
from jax.sharding import PartitionSpec as P

NS_ITERS = 2
BETA_ONE = 0.9
BETA_TWO = 0.9
BETA_STAT = 0.95
EPSILON = 1e-08
NORM_EPS = 1e-06


def contract_rows(left_mat, right_mat):
    return lax.dot_general(
        left_mat, right_mat, (((0,), (0,)), ((), ())), preferred_element_type=jnp.float32
    )


def contract_cols(left_mat, right_mat):
    return lax.dot_general(
        left_mat, right_mat, (((1,), (1,)), ((), ())), preferred_element_type=jnp.float32
    )


def body(group_grads, moment, second, stat_left, stat_right, basis_left, basis_right):
    position = lax.axis_index("shard")
    row_count = moment.shape[0]
    block_width = moment.shape[1]
    local_sum = group_grads[0].astype(jnp.float32)
    summed = lax.psum(local_sum, "dp")
    grad_rows = summed.astype(jnp.bfloat16)
    gradient = lax.all_gather(grad_rows, "shard", axis=0, tiled=True)
    moment_half = (BETA_ONE * moment + (1.0 - BETA_ONE) * grad_rows.astype(jnp.float32)).astype(
        jnp.bfloat16
    )
    left_stat = BETA_STAT * stat_left + (1.0 - BETA_STAT) * contract_cols(grad_rows, gradient)
    grad_cols = lax.dynamic_slice_in_dim(gradient, position * row_count, row_count, 1)
    right_stat = BETA_STAT * stat_right + (1.0 - BETA_STAT) * contract_rows(grad_cols, gradient)
    left_rot, right_rot = (
        lax.all_gather(basis_left.astype(jnp.bfloat16), "shard", axis=0, tiled=True),
        lax.all_gather(basis_right.astype(jnp.bfloat16), "shard", axis=0, tiled=True),
    )
    grad_turned = jnp.dot(grad_rows, right_rot, preferred_element_type=jnp.float32).astype(
        jnp.bfloat16
    )
    moment_turned = jnp.dot(moment_half, right_rot, preferred_element_type=jnp.float32).astype(
        jnp.bfloat16
    )
    grad_block, moment_block = (
        lax.all_to_all(grad_turned, "shard", split_axis=1, concat_axis=0, tiled=True),
        lax.all_to_all(moment_turned, "shard", split_axis=1, concat_axis=0, tiled=True),
    )
    grad_rot = contract_rows(left_rot, grad_block) / block_width
    moment_rot = contract_rows(left_rot, moment_block) / block_width
    second_new = BETA_TWO * second + (1.0 - BETA_TWO) * grad_rot * grad_rot
    scaled = (moment_rot / (jnp.sqrt(second_new) + EPSILON)).astype(jnp.bfloat16)
    turned_back = jnp.dot(left_rot, scaled, preferred_element_type=jnp.float32).astype(jnp.bfloat16)
    back_rows = lax.all_to_all(turned_back, "shard", split_axis=0, concat_axis=1, tiled=True)
    update = (contract_cols(back_rows, right_rot) / block_width).astype(jnp.bfloat16)
    left_product = jnp.dot(
        left_stat.astype(jnp.bfloat16), left_rot, preferred_element_type=jnp.float32
    )
    right_product = jnp.dot(
        right_stat.astype(jnp.bfloat16), right_rot, preferred_element_type=jnp.float32
    )
    left_sq, right_sq = lax.psum(
        (
            jnp.sum(left_product * left_product, axis=0),
            jnp.sum(right_product * right_product, axis=0),
        ),
        "shard",
    )
    left_start = left_product / jnp.sqrt(left_sq / block_width + NORM_EPS)
    right_start = right_product / jnp.sqrt(right_sq / block_width + NORM_EPS)
    left_current = left_start.astype(jnp.bfloat16)
    right_current = right_start.astype(jnp.bfloat16)
    left_result = left_start
    right_result = right_start
    for iteration in range(NS_ITERS):
        left_full, right_full = (
            lax.all_gather(left_current, "shard", axis=0, tiled=True),
            lax.all_gather(right_current, "shard", axis=0, tiled=True),
        )
        left_gram = (contract_cols(left_current, left_full) / block_width).astype(jnp.bfloat16)
        right_gram = (contract_cols(right_current, right_full) / block_width).astype(jnp.bfloat16)
        left_result = 1.5 * left_current.astype(jnp.float32) - 0.5 * jnp.dot(
            left_gram, left_full, preferred_element_type=jnp.float32
        )
        right_result = 1.5 * right_current.astype(jnp.float32) - 0.5 * jnp.dot(
            right_gram, right_full, preferred_element_type=jnp.float32
        )
        if iteration + 1 < NS_ITERS:
            left_current = left_result.astype(jnp.bfloat16)
            right_current = right_result.astype(jnp.bfloat16)
    return (update, second_new, left_result, right_result)


def solution(mesh):
    return jax.shard_map(
        body,
        mesh=mesh,
        in_specs=(
            P("dp", "shard", None),
            P("shard", None),
            P(None, "shard"),
            P("shard", None),
            P("shard", None),
            P("shard", None),
            P("shard", None),
        ),
        out_specs=(P("shard", None), P(None, "shard"), P("shard", None), P("shard", None)),
        check_vma=False,
    )
```

profile of v0, /device:TPU:2, one launch (start us, length us, event | category | flops | bytes accessed | tf_op | source)
XLA Modules:
  0.0 1043.8 jit_solution(8911821349268861389)
XLA Ops:
  7.2 1.9 convert_element_type.88
  9.2 1.0 bitcast_convert_fusion
  10.2 534.5 %all-reduce.2 = bf16[128,1024]{1,0:T(8,128)(2,1)} all-reduce(f32[128,1024]{1,0:T(8,128)S(1)} %bitcast_convert_fusion), channel_id=1, replica_groups=mesh['dp'=64,'shard'=8] {'dp'}, use_global_device_ids=true, to_apply=%region_0.0 | all-reduce | flops 131072 | bytes 786432 | tf_op jit(solution)/shard_map/psum | solution.py:31
  544.8 0.7 convert_element_type.86
  545.6 101.2 %all-gather.12.cloned.1.call-done = bf16[1024,1024]{1,0:T(8,128)(2,1)} async-done(((bf16[128,1024]{1,0:T(8,128)(2,1)}), bf16[1024,1024]{1,0:T(8,128)(2,1)}) %all-gather.12.cloned.1.call-update) | async-done | bytes 2097168 | tf_op jit(solution)/shard_map/all_gather | solution.py:33
  646.8 3.6 multiply_reduce_fusion.1
  650.4 65.8 %all-gather.8.cloned.1.call-done = bf16[1024,1024]{1,0:T(8,128)(2,1)} async-done(((bf16[128,1024]{1,0:T(8,128)(2,1)}), bf16[1024,1024]{1,0:T(8,128)(2,1)}) %all-gather.8.cloned.1.call-update) | async-done | bytes 2097168 | tf_op jit(solution)/shard_map/all_gather | solution.py:42
  716.2 2.6 multiply_reduce_fusion
  718.8 29.0 %all-reduce = (f32[1024]{0:T(1024)S(1)}, f32[1024]{0:T(1024)S(1)}) all-reduce(f32[1024]{0:T(1024)S(1)} %get-tuple-element.16, f32[1024]{0:T(1024)S(1)} %get-tuple-element.18), channel_id=1, replica_groups=mesh['dp'=64,'shard'=8] {'shard'}, use_global_device_ids=true, to_apply=%region_2.0 | all-reduce | flops 2048 | bytes 16384 | tf_op jit(solution)/shard_map/psum | solution.py:67
  747.8 0.8 divide_convert_fusion.1
  748.7 0.8 divide_convert_fusion
  749.5 68.6 %all-gather.14.cloned.1.call-done = bf16[1024,1024]{1,0:T(8,128)(2,1)} async-done(((bf16[128,1024]{1,0:T(8,128)(2,1)}), bf16[1024,1024]{1,0:T(8,128)(2,1)}) %all-gather.14.cloned.1.call-update) | async-done | bytes 2097168 | tf_op jit(solution)/shard_map/all_gather | solution.py:82
  818.1 4.1 fusion.10
  822.7 0.8 copy.25
  823.5 4.9 all-to-all-start.1
  828.5 58.7 %all-gather.18.cloned.1.call-done = bf16[1024,1024]{1,0:T(8,128)(2,1)} async-done(((bf16[128,1024]{1,0:T(8,128)(2,1)}), bf16[1024,1024]{1,0:T(8,128)(2,1)}) %all-gather.18.cloned.1.call-update) | async-done | bytes 2097168 | tf_op jit(solution)/shard_map/all_gather | solution.py:83
  887.2 4.1 fusion.12
  891.8 0.8 copy.26
  892.5 5.1 all-to-all-start
  897.6 1.2 copy.14
  898.9 3.0 bitcast_add_fusion
  901.9 16.0 %all-to-all-done = bf16[128,8,128]{2,0,1:T(8,128)(2,1)S(1)} async-done(((bf16[128,8,128]{2,0,1:T(8,128)(2,1)}), bf16[128,8,128]{2,0,1:T(8,128)(2,1)S(1)}, u32[]{:S(2)}, u32[]{:S(2)}) %all-to-all-start) | async-done | bytes 262176 | tf_op jit(solution)/shard_map/all_to_all | solution.py:52
  917.9 4.4 fusion.20
  922.3 1.7 copy.24
  924.0 3.5 all-to-all-start.2
  927.6 1.0 copy.17
  928.6 25.8 %all-to-all-done.2 = bf16[8,128,128]{1,2,0:T(8,128)(2,1)S(1)} async-done(((bf16[8,128,128]{1,2,0:T(8,128)(2,1)}), bf16[8,128,128]{1,2,0:T(8,128)(2,1)S(1)}, u32[]{:S(2)}, u32[]{:S(2)}) %all-to-all-start.2) | async-done | bytes 262176 | tf_op jit(solution)/shard_map/all_to_all | solution.py:59
  954.3 1.5 fusion.13
  955.9 6.3 all-gather.16.cloned.1.call-done
  962.2 4.1 fusion.3
  966.3 66.5 %all-gather.20.cloned.1.call-done = bf16[1024,1024]{1,0:T(8,128)(2,1)} async-done(((bf16[128,1024]{1,0:T(8,128)(2,1)}), bf16[1024,1024]{1,0:T(8,128)(2,1)}) %all-gather.20.cloned.1.call-update) | async-done | bytes 2097168 | tf_op jit(solution)/shard_map/all_gather | solution.py:83
  1032.8 4.2 fusion
  (40 shorter events, 1.4 us)
Async XLA Ops:
  7.2 537.6 %copy-start.8 = (f32[128,1024]{1,0:T(8,128)S(1)}, f32[128,1024]{1,0:T(8,128)}, u32[]{:S(2)}) copy-start(f32[128,1024]{1,0:T(8,128)} %param.13) | copy-start | bytes 1572868
  7.2 639.6 %copy-start.7 = (f32[128,1024]{1,0:T(8,128)S(1)}, f32[128,1024]{1,0:T(8,128)}, u32[]{:S(2)}) copy-start(f32[128,1024]{1,0:T(8,128)} %param.10) | copy-start | bytes 1572868
  7.2 538.4 %all-gather.10.cloned.1.call-start = ((), (), s32[]{:S(2)}) async-start(), calls=%async_computation.4 | async-start | bytes 2359296 | tf_op jit(solution)/shard_map/all_gather | solution.py:41
  9.1 637.6 %all-gather.12.cloned.1.call-start = ((), (), s32[]{:S(2)}) async-start(), calls=%async_computation.5 | async-start | bytes 2359296 | tf_op jit(solution)/shard_map/all_gather | solution.py:33
  544.7 171.5 %all-gather.8.cloned.1.call-start = ((), (), s32[]{:S(2)}) async-start(), calls=%async_computation.3 | async-start | bytes 2359296 | tf_op jit(solution)/shard_map/all_gather | solution.py:42
  545.5 272.6 %all-gather.14.cloned.1.call-start = ((), (), s32[]{:S(2)}) async-start(), calls=%async_computation.6 | async-start | bytes 2359296 | tf_op jit(solution)/shard_map/all_gather | solution.py:82
  646.8 69.4 %copy-start.1 = (bf16[1024,1024]{1,0:T(8,128)(2,1)S(1)}, bf16[1024,1024]{1,0:T(8,128)(2,1)}, u32[]{:S(2)}) copy-start(bf16[1024,1024]{1,0:T(8,128)(2,1)} %all-gather.12.cloned.1.call-done) | copy-start | bytes 6291460
  748.6 138.6 %all-gather.18.cloned.1.call-start = ((), (), s32[]{:S(2)}) async-start(), calls=%async_computation.8 | async-start | bytes 2359296 | tf_op jit(solution)/shard_map/all_gather | solution.py:83
  749.5 72.8 %copy-start = (bf16[1024,1024]{1,0:T(8,128)(2,1)S(1)}, bf16[1024,1024]{1,0:T(8,128)(2,1)}, u32[]{:S(2)}) copy-start(bf16[1024,1024]{1,0:T(8,128)(2,1)} %all-gather.8.cloned.1.call-done) | copy-start | bytes 6291460
  749.5 72.8 %copy-start.2 = (bf16[128,1024]{1,0:T(8,128)(2,1)S(1)}, bf16[128,1024]{1,0:T(8,128)(2,1)}, u32[]{:S(2)}) copy-start(bf16[128,1024]{1,0:T(8,128)(2,1)} %all-reduce.2) | copy-start | bytes 786436
  749.5 212.7 %all-gather.16.cloned.1.call-start = ((), (), s32[]{:S(2)}) async-start(), calls=%async_computation.7 | async-start | bytes 2359296 | tf_op jit(solution)/shard_map/all_gather | solution.py:82
  822.2 65.0 %copy-start.5 = (bf16[128,1024]{1,0:T(8,128)(2,1)S(1)}, bf16[128,1024]{1,0:T(8,128)(2,1)}, u32[]{:S(2)}) copy-start(bf16[128,1024]{1,0:T(8,128)(2,1)} %divide_convert_fusion) | copy-start | bytes 786436
  823.5 69.0 %all-to-all-start.1 = ((bf16[128,8,128]{2,0,1:T(8,128)(2,1)}), bf16[128,8,128]{2,0,1:T(8,128)(2,1)S(1)}, u32[]{:S(2)}, u32[]{:S(2)}) async-start(bf16[128,8,128]{2,0,1:T(8,128)(2,1)} %bitcast.66), calls=%async_computation.1 | async-start | bytes 524288 | tf_op jit(solution)/shard_map/all_to_all | solution.py:51
  828.4 62.9 %copy-start.9 = (f32[128,1024]{1,0:T(8,128)S(1)}, f32[128,1024]{1,0:T(8,128)}, u32[]{:S(2)}) copy-start(f32[128,1024]{1,0:T(8,128)} %param.8) | copy-start | bytes 1572868
  828.4 204.4 %all-gather.20.cloned.1.call-start = ((), (), s32[]{:S(2)}) async-start(), calls=%async_computation.9 | async-start | bytes 2359296 | tf_op jit(solution)/shard_map/all_gather | solution.py:83
  892.5 6.3 copy-start.6
  892.5 25.3 %all-to-all-start = ((bf16[128,8,128]{2,0,1:T(8,128)(2,1)}), bf16[128,8,128]{2,0,1:T(8,128)(2,1)S(1)}, u32[]{:S(2)}, u32[]{:S(2)}) async-start(bf16[128,8,128]{2,0,1:T(8,128)(2,1)} %bitcast.67), calls=%async_computation | async-start | bytes 524288 | tf_op jit(solution)/shard_map/all_to_all | solution.py:52
  924.0 38.1 %copy-start.3 = (bf16[128,1024]{1,0:T(8,128)(2,1)S(1)}, bf16[128,1024]{1,0:T(8,128)(2,1)}, u32[]{:S(2)}) copy-start(bf16[128,1024]{1,0:T(8,128)(2,1)} %fusion.10) | copy-start | bytes 786436
  924.0 30.3 %all-to-all-start.2 = ((bf16[8,128,128]{1,2,0:T(8,128)(2,1)}), bf16[8,128,128]{1,2,0:T(8,128)(2,1)S(1)}, u32[]{:S(2)}, u32[]{:S(2)}) async-start(bf16[8,128,128]{1,2,0:T(8,128)(2,1)} %bitcast.65), calls=%async_computation.2 | async-start | bytes 524288 | tf_op jit(solution)/shard_map/all_to_all | solution.py:59
  955.9 76.9 %copy-start.4 = (bf16[128,1024]{1,0:T(8,128)(2,1)S(1)}, bf16[128,1024]{1,0:T(8,128)(2,1)}, u32[]{:S(2)}) copy-start(bf16[128,1024]{1,0:T(8,128)(2,1)} %fusion.12) | copy-start | bytes 786436
Sparse Core Ops, SparseCore 0:
  10.7 76.0 all-gather.9
  544.8 101.8 all-gather.11
  649.4 66.7 all-gather.7
  748.7 69.3 all-gather.13
  820.6 66.5 all-gather.17
  889.1 72.9 all-gather.15
  964.2 68.5 all-gather.19
where the time goes:
time: 1040 us
  blocking collectives  563 us (54%)
  waiting for transfers between devices  409 us (39%)
  matrix products  32.6 us (3%)
  between operations  14.3 us (1%)
  starting transfers between devices  13.9 us (1%)
    psum x1, blocking collectives, body(): summed = lax.psum(local_sum, 'dp')  535 us
    all_gather x2, waiting for transfers between devices, body(): lax.all_gather(right_current, 'shard', axis=0, tiled=True)  125 us
    all_gather x1, waiting for transfers between devices, body(): gradient = lax.all_gather(grad_rows, 'shard', axis=0, tiled=True)  101 us
    all_gather x2, waiting for transfers between devices, body(): lax.all_gather(left_current, 'shard', axis=0, tiled=True)  74.9 us
    all_gather x1, waiting for transfers between devices, body(): lax.all_gather(basis_right.astype(jnp.bfloat16), 'shard', axis=0, tiled=T...  65.8 us
    psum x1, blocking collectives, body(): lax.psum((jnp.sum(left_product * left_product, axis=0), jnp.sum(right_pro...  29 us
    all_to_all x1, waiting for transfers between devices, body(): lax.all_to_all(turned_back, 'shard', split_axis=0, concat_axis=1, tiled=T...  25.8 us
  transfers between devices with their start and end apart: 10, of which 8 were waited for; matrix products, arithmetic and copies ran while one was open for 3% of the time, Pallas kernels for 0%

commit v1 on v0

--- a/solution.py
+++ b/solution.py
@@ -28,7 +28,7 @@
     row_count = moment.shape[0]
     block_width = moment.shape[1]
     local_sum = group_grads[0].astype(jnp.float32)
-    summed = lax.psum(local_sum, "dp")
+    summed = jnp.sum(lax.all_gather(local_sum, "dp"), axis=0)
     grad_rows = summed.astype(jnp.bfloat16)
     gradient = lax.all_gather(grad_rows, "shard", axis=0, tiled=True)
     moment_half = (BETA_ONE * moment + (1.0 - BETA_ONE) * grad_rows.astype(jnp.float32)).astype(

time: 1040 us -> 976 us (0.938)
  blocking collectives: 563 us -> 29 us
  waiting for transfers between devices: 409 us -> 862 us
  other arithmetic: 5.11 us -> 18.3 us
    psum x1 -> x0, blocking collectives: 535 us -> none  [body(): summed = lax.psum(local_sum, 'dp')]
    all_gather x0 -> x1, waiting for transfers between devices: none -> 409 us  [body(): summed = jnp.sum(lax.all_gather(local_sum, 'dp'), axis=0)]
    all_gather x1, waiting for transfers between devices: 0.02 us -> 76.4 us  [body(): lax.all_gather(basis_left.astype(jnp.bfloat16), 'shard', axis=0, tiled=True)]
    all_gather x2, waiting for transfers between devices: 125 us -> 74.7 us  [body(): lax.all_gather(right_current, 'shard', axis=0, tiled=True)]
    all_gather x2, waiting for transfers between devices: 74.9 us -> 125 us  [body(): lax.all_gather(left_current, 'shard', axis=0, tiled=True)]
    all_gather x1, waiting for transfers between devices: 101 us -> 69.5 us  [body(): gradient = lax.all_gather(grad_rows, 'shard', axis=0, tiled=True)]
    reduce_sum x0 -> x1, other arithmetic: none -> 12.5 us  [body(): summed = jnp.sum(lax.all_gather(local_sum, 'dp'), axis=0)]
  transfers between devices with their start and end apart: 10 -> 11, of which waited for: 8 -> 10; matrix products, arithmetic and copies ran while one was open for 3% -> 5% of each run, Pallas kernels for 0% -> 0%
where the time goes in v1:
time: 976 us
  waiting for transfers between devices  862 us (88%)
  matrix products  32.7 us (3%)
  blocking collectives  29 us (3%)
  other arithmetic  18.3 us (2%)
  between operations  14.3 us (1%)
  starting transfers between devices  13.9 us (1%)
    all_gather x1, waiting for transfers between devices, body(): summed = jnp.sum(lax.all_gather(local_sum, 'dp'), axis=0)  409 us
    all_gather x2, waiting for transfers between devices, body(): lax.all_gather(left_current, 'shard', axis=0, tiled=True)  125 us
    all_gather x1, waiting for transfers between devices, body(): lax.all_gather(basis_left.astype(jnp.bfloat16), 'shard', axis=0, tiled=True)  76.4 us
    all_gather x2, waiting for transfers between devices, body(): lax.all_gather(right_current, 'shard', axis=0, tiled=True)  74.7 us
    all_gather x1, waiting for transfers between devices, body(): gradient = lax.all_gather(grad_rows, 'shard', axis=0, tiled=True)  69.5 us
    all_gather x1, waiting for transfers between devices, body(): lax.all_gather(basis_right.astype(jnp.bfloat16), 'shard', axis=0, tiled=T...  65.6 us
    psum x1, blocking collectives, body(): lax.psum((jnp.sum(left_product * left_product, axis=0), jnp.sum(right_pro...  29 us
    all_to_all x1, waiting for transfers between devices, body(): lax.all_to_all(turned_back, 'shard', split_axis=0, concat_axis=1, tiled=T...  25.5 us
  transfers between devices with their start and end apart: 11, of which 10 were waited for; matrix products, arithmetic and copies ran while one was open for 5% of the time, Pallas kernels for 0%

profile of v1, /device:TPU:2, one launch (start us, length us, event | category | flops | bytes accessed | tf_op | source)
XLA Modules:
  0.0 975.7 jit_solution(9007732347562431505)
XLA Ops:
  7.2 1.8 convert_element_type.79
  9.1 1.8 convert_element_type.85
  11.0 408.7 %all-gather.9.cloned.1.call-done = f32[64,128,1024]{2,1,0:T(8,128)} async-done(((f32[1,128,1024]{2,1,0:T(8,128)}), f32[64,128,1024]{2,1,0:T(8,128)}) %all-gather.9.cloned.1.call-update) | async-done | bytes 33554448 | tf_op jit(solution)/shard_map/all_gather | solution.py:31
  419.7 12.5 %reduce_sum.27 = bf16[128,1024]{1,0:T(8,128)(2,1)} reduce(f32[64,128,1024]{2,1,0:T(8,128)} %all-gather.9.cloned.1.call-done, f32[]{:T(128)} %constant.16.clone.1), dimensions={0}, to_apply=%region_0.0 | reduce | flops 8257536 | bytes 33816580 | tf_op jit(solution)/shard_map/reduce_sum | solution.py:31
  433.1 76.4 %all-gather.13.cloned.1.call-done = bf16[1024,1024]{1,0:T(8,128)(2,1)} async-done(((bf16[128,1024]{1,0:T(8,128)(2,1)}), bf16[1024,1024]{1,0:T(8,128)(2,1)}) %all-gather.13.cloned.1.call-update) | async-done | bytes 2097168 | tf_op jit(solution)/shard_map/all_gather | solution.py:41
  509.5 69.5 %all-gather.15.cloned.1.call-done = bf16[1024,1024]{1,0:T(8,128)(2,1)} async-done(((bf16[128,1024]{1,0:T(8,128)(2,1)}), bf16[1024,1024]{1,0:T(8,128)(2,1)}) %all-gather.15.cloned.1.call-update) | async-done | bytes 2097168 | tf_op jit(solution)/shard_map/all_gather | solution.py:33
  579.0 3.6 multiply_reduce_fusion.1
  582.6 65.6 %all-gather.11.cloned.1.call-done = bf16[1024,1024]{1,0:T(8,128)(2,1)} async-done(((bf16[128,1024]{1,0:T(8,128)(2,1)}), bf16[1024,1024]{1,0:T(8,128)(2,1)}) %all-gather.11.cloned.1.call-update) | async-done | bytes 2097168 | tf_op jit(solution)/shard_map/all_gather | solution.py:42
  648.2 2.6 multiply_reduce_fusion
  650.9 29.0 %all-reduce = (f32[1024]{0:T(1024)S(1)}, f32[1024]{0:T(1024)S(1)}) all-reduce(f32[1024]{0:T(1024)S(1)} %get-tuple-element.20, f32[1024]{0:T(1024)S(1)} %get-tuple-element.22), channel_id=1, replica_groups=mesh['dp'=64,'shard'=8] {'shard'}, use_global_device_ids=true, to_apply=%region_2.0 | all-reduce | flops 2048 | bytes 16384 | tf_op jit(solution)/shard_map/psum | solution.py:67
  679.9 0.8 divide_convert_fusion
  680.7 0.8 divide_convert_fusion.1
  681.6 68.6 %all-gather.21.cloned.1.call-done = bf16[1024,1024]{1,0:T(8,128)(2,1)} async-done(((bf16[128,1024]{1,0:T(8,128)(2,1)}), bf16[1024,1024]{1,0:T(8,128)(2,1)}) %all-gather.21.cloned.1.call-update) | async-done | bytes 2097168 | tf_op jit(solution)/shard_map/all_gather | solution.py:83
  750.1 4.2 fusion.12
  754.8 0.8 copy.30
  755.6 4.9 all-to-all-start.1
  760.6 58.7 %all-gather.17.cloned.1.call-done = bf16[1024,1024]{1,0:T(8,128)(2,1)} async-done(((bf16[128,1024]{1,0:T(8,128)(2,1)}), bf16[1024,1024]{1,0:T(8,128)(2,1)}) %all-gather.17.cloned.1.call-update) | async-done | bytes 2097168 | tf_op jit(solution)/shard_map/all_gather | solution.py:82
  819.3 4.1 fusion.10
  824.6 5.1 all-to-all-start
  829.7 1.2 copy.19
  831.0 3.0 bitcast_add_fusion
  833.9 16.4 %all-to-all-done = bf16[128,8,128]{2,0,1:T(8,128)(2,1)S(1)} async-done(((bf16[128,8,128]{2,0,1:T(8,128)(2,1)}), bf16[128,8,128]{2,0,1:T(8,128)(2,1)S(1)}, u32[]{:S(2)}, u32[]{:S(2)}) %all-to-all-start) | async-done | bytes 262176 | tf_op jit(solution)/shard_map/all_to_all | solution.py:52
  850.3 4.4 fusion.20
  854.8 1.7 copy.29
  856.5 3.5 all-to-all-start.2
  860.0 1.0 copy.22
  861.0 25.5 %all-to-all-done.2 = bf16[8,128,128]{1,2,0:T(8,128)(2,1)S(1)} async-done(((bf16[8,128,128]{1,2,0:T(8,128)(2,1)}), bf16[8,128,128]{1,2,0:T(8,128)(2,1)S(1)}, u32[]{:S(2)}, u32[]{:S(2)}) %all-to-all-start.2) | async-done | bytes 262176 | tf_op jit(solution)/shard_map/all_to_all | solution.py:59
  886.5 1.5 fusion.13
  888.0 6.1 all-gather.23.cloned.1.call-done
  894.2 4.1 fusion
  898.3 66.4 %all-gather.19.cloned.1.call-done = bf16[1024,1024]{1,0:T(8,128)(2,1)} async-done(((bf16[128,1024]{1,0:T(8,128)(2,1)}), bf16[1024,1024]{1,0:T(8,128)(2,1)}) %all-gather.19.cloned.1.call-update) | async-done | bytes 2097168 | tf_op jit(solution)/shard_map/all_gather | solution.py:82
  964.7 4.2 fusion.3
  (43 shorter events, 2.9 us)
Async XLA Ops:
  7.2 412.5 %all-gather.9.cloned.1.call-start = ((), (), s32[]{:S(2)}) async-start(), calls=%async_computation.3 | async-start | bytes 34078720 | tf_op jit(solution)/shard_map/all_gather | solution.py:31
  9.0 500.4 %all-gather.13.cloned.1.call-start = ((), (), s32[]{:S(2)}) async-start(), calls=%async_computation.5 | async-start | bytes 2359296 | tf_op jit(solution)/shard_map/all_gather | solution.py:41
  10.9 421.4 %copy-start.8 = (f32[128,1024]{1,0:T(8,128)S(1)}, f32[128,1024]{1,0:T(8,128)}, u32[]{:S(2)}) copy-start(f32[128,1024]{1,0:T(8,128)} %param.13) | copy-start | bytes 1572868
  10.9 568.1 %copy-start.7 = (f32[128,1024]{1,0:T(8,128)S(1)}, f32[128,1024]{1,0:T(8,128)}, u32[]{:S(2)}) copy-start(f32[128,1024]{1,0:T(8,128)} %param.10) | copy-start | bytes 1572868
  10.9 568.0 %all-gather.15.cloned.1.call-start = ((), (), s32[]{:S(2)}) async-start(), calls=%async_computation.6 | async-start | bytes 2359296 | tf_op jit(solution)/shard_map/all_gather | solution.py:33
  432.2 216.0 %all-gather.11.cloned.1.call-start = ((), (), s32[]{:S(2)}) async-start(), calls=%async_computation.4 | async-start | bytes 2359296 | tf_op jit(solution)/shard_map/all_gather | solution.py:42
  433.0 317.1 %all-gather.21.cloned.1.call-start = ((), (), s32[]{:S(2)}) async-start(), calls=%async_computation.9 | async-start | bytes 2359296 | tf_op jit(solution)/shard_map/all_gather | solution.py:83
  579.0 69.3 %copy-start.1 = (bf16[1024,1024]{1,0:T(8,128)(2,1)S(1)}, bf16[1024,1024]{1,0:T(8,128)(2,1)}, u32[]{:S(2)}) copy-start(bf16[1024,1024]{1,0:T(8,128)(2,1)} %all-gather.15.cloned.1.call-done) | copy-start | bytes 6291460
  680.7 138.6 %all-gather.17.cloned.1.call-start = ((), (), s32[]{:S(2)}) async-start(), calls=%async_computation.7 | async-start | bytes 2359296 | tf_op jit(solution)/shard_map/all_gather | solution.py:82
  681.5 72.8 %copy-start = (bf16[1024,1024]{1,0:T(8,128)(2,1)S(1)}, bf16[1024,1024]{1,0:T(8,128)(2,1)}, u32[]{:S(2)}) copy-start(bf16[1024,1024]{1,0:T(8,128)(2,1)} %all-gather.11.cloned.1.call-done) | copy-start | bytes 6291460
  681.5 72.8 %copy-start.2 = (bf16[128,1024]{1,0:T(8,128)(2,1)S(1)}, bf16[128,1024]{1,0:T(8,128)(2,1)}, u32[]{:S(2)}) copy-start(bf16[128,1024]{1,0:T(8,128)(2,1)} %reduce_sum.27) | copy-start | bytes 786436
  681.5 212.6 %all-gather.23.cloned.1.call-start = ((), (), s32[]{:S(2)}) async-start(), calls=%async_computation.10 | async-start | bytes 2359296 | tf_op jit(solution)/shard_map/all_gather | solution.py:83
  754.3 65.0 %copy-start.5 = (bf16[128,1024]{1,0:T(8,128)(2,1)S(1)}, bf16[128,1024]{1,0:T(8,128)(2,1)}, u32[]{:S(2)}) copy-start(bf16[128,1024]{1,0:T(8,128)(2,1)} %divide_convert_fusion.1) | copy-start | bytes 786436
  755.6 69.0 %all-to-all-start.1 = ((bf16[128,8,128]{2,0,1:T(8,128)(2,1)}), bf16[128,8,128]{2,0,1:T(8,128)(2,1)S(1)}, u32[]{:S(2)}, u32[]{:S(2)}) async-start(bf16[128,8,128]{2,0,1:T(8,128)(2,1)} %bitcast.63), calls=%async_computation.1 | async-start | bytes 524288 | tf_op jit(solution)/shard_map/all_to_all | solution.py:51
  760.5 62.9 %copy-start.9 = (f32[128,1024]{1,0:T(8,128)S(1)}, f32[128,1024]{1,0:T(8,128)}, u32[]{:S(2)}) copy-start(f32[128,1024]{1,0:T(8,128)} %param.8) | copy-start | bytes 1572868
  760.5 204.2 %all-gather.19.cloned.1.call-start = ((), (), s32[]{:S(2)}) async-start(), calls=%async_computation.8 | async-start | bytes 2359296 | tf_op jit(solution)/shard_map/all_gather | solution.py:82
  824.6 6.3 copy-start.6
  824.6 25.7 %all-to-all-start = ((bf16[128,8,128]{2,0,1:T(8,128)(2,1)}), bf16[128,8,128]{2,0,1:T(8,128)(2,1)S(1)}, u32[]{:S(2)}, u32[]{:S(2)}) async-start(bf16[128,8,128]{2,0,1:T(8,128)(2,1)} %bitcast.64), calls=%async_computation | async-start | bytes 524288 | tf_op jit(solution)/shard_map/all_to_all | solution.py:52
  856.5 37.7 %copy-start.3 = (bf16[128,1024]{1,0:T(8,128)(2,1)S(1)}, bf16[128,1024]{1,0:T(8,128)(2,1)}, u32[]{:S(2)}) copy-start(bf16[128,1024]{1,0:T(8,128)(2,1)} %fusion.12) | copy-start | bytes 786436
  856.5 30.0 %all-to-all-start.2 = ((bf16[8,128,128]{1,2,0:T(8,128)(2,1)}), bf16[8,128,128]{1,2,0:T(8,128)(2,1)S(1)}, u32[]{:S(2)}, u32[]{:S(2)}) async-start(bf16[8,128,128]{1,2,0:T(8,128)(2,1)} %bitcast.62), calls=%async_computation.2 | async-start | bytes 524288 | tf_op jit(solution)/shard_map/all_to_all | solution.py:59
  888.0 76.7 %copy-start.4 = (bf16[128,1024]{1,0:T(8,128)(2,1)S(1)}, bf16[128,1024]{1,0:T(8,128)(2,1)}, u32[]{:S(2)}) copy-start(bf16[128,1024]{1,0:T(8,128)(2,1)} %fusion.10) | copy-start | bytes 786436
Sparse Core Ops, SparseCore 0:
  12.9 406.7 all-gather.8
  422.3 87.0 all-gather.12
  512.1 66.7 all-gather.14
  581.5 66.7 all-gather.10
  680.8 69.3 all-gather.20
  752.6 66.5 all-gather.16
  821.3 72.7 all-gather.22
  896.2 68.4 all-gather.18
